TPU v7x, 256 devices: a whole 4x4x8 slice. The times are simulated.
256 devices in a mesh: curves: 64 (over y, z_hi, x, core), primes: 4 (over z_lo).
Axes of the slice: x: 4, y: 4, z: 8 (z_hi: 2, z_lo: 4; z = z_hi * 4 + z_lo), core: 2. Of those that a mesh axis runs over, the one named last changes fastest.
Arguments:
- traces: int32 [32768, 24576], P('curves', 'primes'), may hold values from -724 to 724, as said below
- primes: int32 [24576], P('primes'), may hold values from 2 to 131071, as said below
- family: int32 [32768], P('curves'), may hold values from 0 to 1023
- log_conductor: float32 [32768], P('curves'), may hold values from 8 to 24
Outputs:
- profile: float32 [1024, 256], P('curves')
Inputs may be any that keep to these rules, and one draw needn't show every extreme that they name: `primes`: every value is a prime below 131072. traces[c, k] squared is at most 4 primes[k].
All inputs are finite; a program needn't handle non-finite values.
Results may differ from a plain program's by a relative error of at most 0.0038.
Values sent between devices are 32-bit elements; how exact they have to be, the bound alone decides.
A program may use at most 64 MiB of HBM per device.

v0:
```python
import jax
import jax.numpy as jnp
from jax import lax
from jax.sharding import PartitionSpec as P

HEIGHTS = 128
FAM_DEV = 16


def on_device(traces, primes, family, log_conductor):
    log_prime = jnp.log(primes.astype(jnp.float32))
    heights = (lax.iota(jnp.float32, HEIGHTS) + 1.0) * 0.5
    angles = log_prime[:, None] * heights[None, :]
    tables = jnp.concatenate([jnp.cos(angles), jnp.sin(angles)], axis=1).astype(jnp.bfloat16)
    weight = log_prime / primes.astype(jnp.float32)
    coefficient = (traces.astype(jnp.float32) * weight[None, :]).astype(jnp.bfloat16)
    partial_value = jnp.dot(coefficient, tables, preferred_element_type=jnp.float32)
    factor = (-2.0 / log_conductor)[:, None]
    families = lax.axis_size("curves") * FAM_DEV
    onehot = (family[:, None] == lax.iota(jnp.int32, families)[None, :]).astype(jnp.float32)
    local_counts = jnp.sum(onehot, axis=0)
    totals = lax.psum(partial_value, "primes")
    profile_sums = lax.psum_scatter(
        lax.dot_general(
            onehot,
            totals * factor,
            (((0,), (0,)), ((), ())),
            precision=lax.Precision.HIGHEST,
            preferred_element_type=jnp.float32,
        ),
        "curves",
        scatter_dimension=0,
        tiled=True,
    )
    counts = lax.psum_scatter(local_counts, "curves", scatter_dimension=0, tiled=True)
    return profile_sums / jnp.sqrt(jnp.maximum(counts, 1.0))[:, None]


def solution(mesh):
    return jax.shard_map(
        on_device,
        mesh=mesh,
        in_specs=(P("curves", "primes"), P("primes"), P("curves"), P("curves")),
        out_specs=P("curves", None),
        check_vma=False,
    )
```

profile of v0, /device:TPU:1, one launch (start us, length us, event | category | flops | bytes accessed | tf_op | source)
XLA Modules:
  0.0 497.8 jit_solution(10045084237696348343)
XLA Ops:
  6.5 0.0 all-reduce.3.cloned.1.call-start
  6.5 0.8 convert_log_fusion
  7.3 12.3 %fusion.2 = (bf16[6144,128]{1,0:T(8,128)(2,1)S(1)}, bf16[6144,128]{1,0:T(8,128)(2,1)S(1)}) fusion(f32[128]{0:T(128)S(1)} %add_multiply_fusion, f32[6144]{0:T(1024)S(1)} %get-tuple-element.7), kind=kLoop, calls=%fused_computation.5 | loop fusion | flops 2359296 | bytes 3170816 | tf_op jit(solution)/shard_map/convert
  19.6 0.0 copy-start.1
  19.6 0.0 copy-start
  19.7 7.3 %fusion = f32[512,256]{1,0:T(8,128)} fusion(s32[512,6144]{1,0:T(8,128)} %param.4, f32[6144]{0:T(1024)S(1)} %get-tuple-element.8, bf16[6144,128]{1,0:T(8,128)(2,1)S(1)} %get-tuple-element.6, bf16[6144,128]{1,0:T(8,128)(2,1)S(1)} %get-tuple-element.5), kind=kOutput, calls=%fused_computation.1 | convolution fusion | flops 1626341376 | bytes 16277504 | tf_op jit(solution)/shard_map/dot_general | solution.py:17
  26.9 0.0 copy-start.2
  26.9 0.0 all-reduce.3.cloned.1.call-update
  27.0 0.0 reduce-scatter.2.cloned.1.call-start
  27.0 0.0 copy-done.1
  27.0 54.2 %all-reduce.3.cloned.1.call-done = f32[512,256]{1,0:T(8,128)} async-done(((f32[512,256]{1,0:T(8,128)}), f32[512,256]{1,0:T(8,128)}) %all-reduce.3.cloned.1.call-update) | async-done | bytes 524304 | tf_op jit(solution)/shard_map/psum | solution.py:22
  81.2 0.0 copy-done
  81.2 4.0 fusion.7
  85.3 0.0 reduce-scatter.2.cloned.1.call-update
  85.3 0.0 copy-done.2
  85.3 0.6 dynamic-slice
  86.5 0.3 convert_reduce_fusion
  86.8 203.1 %all-reduce = f32[1024]{0:T(1024)S(1)} all-reduce(f32[1024]{0:T(1024)S(1)} %convert_reduce_fusion), channel_id=3, replica_groups=mesh['curves'=64,'primes'=4] {'curves'}, use_global_device_ids=true, to_apply=%region_3.0.clone | all-reduce | flops 1024 | bytes 8192
  289.9 0.1 fusion.11
  289.9 199.6 %reduce-scatter.2.cloned.1.call-done = f32[16,256]{1,0:T(8,128)} async-done(((f32[1024,256]{1,0:T(8,128)}), f32[16,256]{1,0:T(8,128)}) %reduce-scatter.2.cloned.1.call-update) | async-done | bytes 16400 | tf_op jit(solution)/shard_map/reduce_scatter | solution.py:23
  489.5 1.4 broadcast_divide_fusion
  (2 shorter events, 0.0 us)
Async XLA Ops:
  6.5 74.7 %all-reduce.3.cloned.1.call-start = ((), (), s32[]{:S(2)}) async-start(), calls=%async_computation.1 | async-start | bytes 1048576 | tf_op jit(solution)/shard_map/psum | solution.py:22
  19.6 7.4 %copy-start.1 = (f32[512]{0:T(512)S(1)}, f32[512]{0:T(512)}, u32[]{:S(2)}) copy-start(f32[512]{0:T(512)} %param.7) | copy-start | bytes 6148
  19.6 61.6 %copy-start = (s32[512]{0:T(512)S(1)}, s32[512]{0:T(512)}, u32[]{:S(2)}) copy-start(s32[512]{0:T(512)} %param.6) | copy-start | bytes 6148
  26.9 58.3 %copy-start.2 = (u32[256]{0:T(256)S(1)}, u32[256]{0:T(256)}, u32[]{:S(2)}) copy-start(u32[256]{0:T(256)} %constant.11) | copy-start | bytes 3076
  27.0 462.6 %reduce-scatter.2.cloned.1.call-start = ((), (), s32[]{:S(2)}) async-start(), calls=%async_computation.2 | async-start | bytes 1064960 | tf_op jit(solution)/shard_map/reduce_scatter | solution.py:23
Sparse Core Ops, SparseCore 0:
  27.1 54.1 all-reduce.2
  85.4 404.0 reduce-scatter.1
where the time goes:
time: 506 us; the launch traced here: 498 us
  waiting for transfers between devices  254 us (50%)
  blocking collectives  203 us (40%)
  other arithmetic  14.8 us (3%)
  between operations  14.1 us (3%)
  matrix products  11.3 us (2%)
    unnamed x1, blocking collectives  203 us
    reduce_scatter x1, waiting for transfers between devices, on_device(): lax.psum_scatter(lax.dot_general(onehot, totals * factor, (((0,), (0,)),...  200 us
    psum x1, waiting for transfers between devices, on_device(): totals = lax.psum(partial_value, 'primes')  54.2 us
    another operation x1, other arithmetic  12.3 us
  transfers between devices with their start and end apart: 2, of which 2 were waited for; matrix products, arithmetic and copies ran while one was open for 0% of the time, Pallas kernels for 0%

commit v1 on v0

v1 whole, which is shorter than its diff:
```python
import jax
import jax.numpy as jnp
from jax import lax
from jax.experimental import pallas as pl
from jax.experimental.pallas import tpu as pltpu
from jax.sharding import PartitionSpec as P

MESH = pl.DeviceIdType.MESH
HEIGHTS = 128
ROWS = 512
DEPTH = 6144
CHUNK = 1024
STEPS = DEPTH // CHUNK
GROUPS = CHUNK // 128
FAMILIES = 1024
F32 = jnp.float32
BF16 = jnp.bfloat16


def times(a, b):
    return a[0] * b[0] - a[1] * b[1], a[0] * b[1] + a[1] * b[0]


def one_hot(cond):
    return jnp.where(cond, 1.0, 0.0).astype(BF16)


def kernel(
    traces, primes, family, conductor, out,
    tr, base_cos, base_sin, weight, table, total, factor, hot, rhs, send0, recv0, family2,
    sendx0, sendx1, recvx0, recvx1, sendy0, sendy1, recvy0, recvy1, sendz, recvz,
    copy_sem, ssem0, rsem0, ssem1, rsem1, ssem2, rsem2, ssem3, rsem3,
):
    me = lax.axis_index("curves")
    zl = lax.axis_index("primes")
    core = lax.rem(me, 2)
    x = lax.rem(lax.div(me, 2), 4)
    zh = lax.rem(lax.div(me, 8), 2)
    y = lax.div(me, 16)

    def curve(y, zh, x, core):
        return ((y * 2 + zh) * 4 + x) * 2 + core

    def along_x(p):
        return (curve(y, zh, lax.rem(x + p, 4), core), zl)

    def along_y(p):
        return (curve(lax.rem(y + p, 4), zh, x, core), zl)

    spot = (zh * 4 + zl) * 2 + core

    def along_z(p):
        q = lax.rem(spot + p, 16)
        return (curve(y, lax.div(q, 8), x, lax.rem(q, 2)), lax.rem(lax.div(q, 2), 4)), q

    sibling = (curve(y, zh, x, 1 - core), zl)

    def fetch(i):
        return pltpu.make_async_copy(traces.at[:, pl.ds(i * CHUNK, CHUNK)], tr.at[i], copy_sem.at[i])

    for i in range(STEPS):
        fetch(i).start()

    barrier = pltpu.get_barrier_semaphore()
    peers = [along_x(p) for p in (1, 2, 3)] + [along_y(p) for p in (1, 2, 3)] + [along_z(p)[0] for p in range(1, 16)]
    for peer in peers:
        pl.semaphore_signal(barrier, inc=1, device_id=peer, device_id_type=MESH)

    prime = primes[...].astype(F32)
    log_prime = jnp.log(prime)
    weight[...] = log_prime / prime
    base_cos[...] = jnp.cos(log_prime * 0.5)
    base_sin[...] = jnp.sin(log_prime * 0.5)
    total[...] = jnp.zeros_like(total)

    def labels(half):
        at = lax.broadcasted_iota(jnp.int32, (512, 128), 0)
        r, k, h = at & 7, (at >> 3) & 1, (at >> 4) & 1
        second, first = (at >> 5) & 3, (at >> 7) & 3
        xs, ys = (first, second) if half == 0 else (second, first)
        return (((ys * 2 + h) * 4 + xs) * 2 + k) * 16 + half * 8 + r

    label = [labels(0), labels(1)]

    def fill_hot(ref, base):
        for g in range(4):
            row = jnp.broadcast_to(ref[g:g + 1, :], (512, 128))
            for half in (0, 1):
                hot[half * 512:half * 512 + 512, (base + g) * 128:(base + g) * 128 + 128] = one_hot(label[half] == row)

    fill_hot(family, 0)
    inverse = -2.0 / conductor[...]
    for g in range(4):
        factor[g * 128:g * 128 + 128, :] = jnp.transpose(jnp.broadcast_to(inverse[g:g + 1, :], (128, 128)))

    sub = lax.broadcasted_iota(jnp.int32, (8, 128), 0)
    bits = [(sub & 1) != 0, (sub & 2) != 0, (sub & 4) != 0]

    def pick(mask, a):
        return jnp.where(mask, a[0], 1.0), jnp.where(mask, a[1], 0.0)

    def tables(row, lane):
        z = (jnp.broadcast_to(base_cos[pl.ds(row, 1), :], (8, 128)), jnp.broadcast_to(base_sin[pl.ds(row, 1), :], (8, 128)))
        z2 = times(z, z)
        z4 = times(z2, z2)
        powers = [times(times(z, pick(bits[0], z)), times(pick(bits[1], z2), pick(bits[2], z4)))]
        step = times(z4, z4)
        for _ in range(4):
            powers = powers + [times(a, step) for a in powers]
            step = times(step, step)
        for q in range(0, 16, 2):
            for part in (0, 1):
                both = jnp.concatenate([powers[q][part], powers[q + 1][part]], axis=0)
                table[part * 128 + q * 8:part * 128 + q * 8 + 16, lane:lane + 128] = both.astype(BF16)

    def trace_step(i, carry):
        for g in range(GROUPS):
            tables(i * GROUPS + g, g * 128)
        fetch(i).wait()
        w = jnp.concatenate([weight[pl.ds(i * GROUPS + g, 1), :] for g in range(GROUPS)], axis=1)
        coefficient = (tr[i].astype(F32) * w).astype(BF16)
        total[...] += lax.dot_general(coefficient, table[...], (((1,), (1,)), ((), ())), preferred_element_type=F32)
        return carry

    lax.fori_loop(0, STEPS - 1, trace_step, 0)

    pl.semaphore_wait(barrier, len(peers))
    families = pltpu.make_async_remote_copy(
        family, family2, ssem0.at[0], rsem0.at[0], device_id=sibling, device_id_type=MESH
    )
    families.start()
    trace_step(STEPS - 1, 0)

    def density(k):
        return total[:, pl.ds(pl.multiple_of(k * 128, 128), 128)] * factor[...]

    send0[...] = density(1 - core)
    columns = pltpu.make_async_remote_copy(
        send0, recv0, ssem0.at[1], rsem0.at[1], device_id=sibling, device_id_type=MESH
    )
    columns.start()

    def split(value, base):
        high = value.astype(BF16)
        rhs[base:base + 512, 0:128] = high
        rhs[base:base + 512, 128:256] = (value - high.astype(F32)).astype(BF16)

    split(density(core), 0)
    families.wait()
    fill_hot(family2, 4)

    counts = jnp.zeros((8, 128), F32)
    for ref in (family, family2):
        for g in range(4):
            row = ref[g:g + 1, :]
            high = one_hot(lax.broadcasted_iota(jnp.int32, (8, 128), 0) == (row >> 7))
            low = one_hot(lax.broadcasted_iota(jnp.int32, (128, 128), 0) == (row & 127))
            counts += lax.dot_general(high, low, (((1,), (1,)), ((), ())), preferred_element_type=F32)

    columns.wait()
    split(recv0[...], 512)

    def family_sums(half, block):
        at = pl.multiple_of(half * 512 + block * 128, 128)
        both = lax.dot_general(hot[pl.ds(at, 128), :], rhs[...], (((1,), (0,)), ((), ())), preferred_element_type=F32)
        return both[:, 0:128] + both[:, 128:256]

    def exchange(send, recv, half, p, ssem, rsem, device):
        return pltpu.make_async_remote_copy(
            send.at[p - 1], recv.at[p - 1], ssem.at[half, p - 1], rsem.at[half, p - 1],
            device_id=device, device_id_type=MESH,
        )

    first = {}
    for p in (2, 1, 3):
        sendx0[p - 1, 0:128, :] = family_sums(0, lax.rem(x + p, 4))
        sendx0[p - 1, 128:136, :] = counts
        first[0, p] = exchange(sendx0, recvx0, 0, p, ssem1, rsem1, along_x(p))
        first[0, p].start()
        sendx1[p - 1, 0:128, :] = family_sums(1, lax.rem(y + p, 4))
        first[1, p] = exchange(sendx1, recvx1, 1, p, ssem1, rsem1, along_y(p))
        first[1, p].start()
    recvx0[3, 0:128, :] = family_sums(0, x)
    recvx0[3, 128:136, :] = counts
    recvx1[3, 0:128, :] = family_sums(1, y)

    second = {}
    for half in (0, 1):
        recv, send, other, into, device = (
            (recvx0, sendy0, y, recvy0, along_y) if half == 0 else (recvx1, sendy1, x, recvy1, along_x)
        )
        for p in (1, 2, 3):
            first[half, p].wait()
        if half == 0:
            counts = recv[0, 128:136, :] + recv[1, 128:136, :] + recv[2, 128:136, :] + recv[3, 128:136, :]

        def block(b):
            at = pl.ds(pl.multiple_of(b * 32, 32), 32)
            return (recv[0, at, :] + recv[1, at, :]) + (recv[2, at, :] + recv[3, at, :])

        for p in (2, 1, 3):
            send[p - 1, 0:32, :] = block(lax.rem(other + p, 4))
            if half == 0:
                send[p - 1, 32:40, :] = counts
            second[half, p] = exchange(send, into, half, p, ssem2, rsem2, device(p))
            second[half, p].start()
        into[3, 0:32, :] = block(other)
        if half == 0:
            into[3, 32:40, :] = counts

    for half in (0, 1):
        recv = (recvy0, recvy1)[half]
        for p in (1, 2, 3):
            second[half, p].wait()
        value = (recv[0] + recv[1]) + (recv[2] + recv[3])
        for b in range(4):
            sendz[b, half * 8:half * 8 + 8, :] = value[b * 8:b * 8 + 8, :]
            if half == 0:
                sendz[b, 16:24, :] = value[32:40, :]

    third = []
    for p in list(range(1, 16)):
        device, q = along_z(p)
        block = lax.div(q, 8) * 2 + lax.rem(q, 2)
        copy = pltpu.make_async_remote_copy(
            sendz.at[block], recvz.at[spot], ssem3.at[p], rsem3.at[spot], device_id=device, device_id_type=MESH
        )
        copy.start()
        third.append(copy)
    recvz[spot] = sendz[zh * 2 + core]
    for p in range(1, 16):
        q = lax.rem(spot + p, 16)
        pltpu.make_async_remote_copy(
            sendz.at[0], recvz.at[q], ssem3.at[p], rsem3.at[q], device_id=sibling, device_id_type=MESH
        ).wait_recv()
    for copy in third:
        copy.wait_send()

    count_row = recvz[0, pl.ds(16 + lax.div(me, 8), 1), :] + recvz[8, pl.ds(16 + lax.div(me, 8), 1), :]
    lane = lax.broadcasted_iota(jnp.int32, (16, 128), 1)
    want = lax.broadcasted_iota(jnp.int32, (16, 128), 0) + lax.rem(me, 8) * 16
    count = jnp.sum(jnp.where(lane == want, jnp.broadcast_to(count_row, (16, 128)), 0.0), axis=1, keepdims=True)
    norm = 1.0 / jnp.sqrt(jnp.maximum(count, 1.0))
    for k in (0, 1):
        value = recvz[k, 0:16, :]
        for s in range(1, 8):
            value = value + recvz[2 * s + k, 0:16, :]
        out[:, k * 128:k * 128 + 128] = value * norm


def on_device(traces, primes, family, log_conductor):
    vmem = pl.BlockSpec(memory_space=pltpu.VMEM)
    dma = pltpu.SemaphoreType.DMA
    return pl.pallas_call(
        kernel,
        out_shape=jax.ShapeDtypeStruct((16, 256), F32),
        in_specs=[pl.BlockSpec(memory_space=pl.ANY), vmem, vmem, vmem],
        out_specs=vmem,
        scratch_shapes=[
            pltpu.VMEM((STEPS, ROWS, CHUNK), jnp.int32),
            pltpu.VMEM((48, 128), F32),
            pltpu.VMEM((48, 128), F32),
            pltpu.VMEM((48, 128), F32),
            pltpu.VMEM((256, CHUNK), BF16),
            pltpu.VMEM((ROWS, 256), F32),
            pltpu.VMEM((ROWS, 128), F32),
            pltpu.VMEM((FAMILIES, 1024), BF16),
            pltpu.VMEM((1024, 256), BF16),
            pltpu.VMEM((ROWS, 128), F32),
            pltpu.VMEM((ROWS, 128), F32),
            pltpu.VMEM((4, 128), jnp.int32),
            pltpu.VMEM((3, 136, 128), F32),
            pltpu.VMEM((3, 128, 128), F32),
            pltpu.VMEM((4, 136, 128), F32),
            pltpu.VMEM((4, 128, 128), F32),
            pltpu.VMEM((3, 40, 128), F32),
            pltpu.VMEM((3, 32, 128), F32),
            pltpu.VMEM((4, 40, 128), F32),
            pltpu.VMEM((4, 32, 128), F32),
            pltpu.VMEM((4, 24, 128), F32),
            pltpu.VMEM((16, 24, 128), F32),
            dma((STEPS,)),
            dma((2,)),
            dma((2,)),
            dma((2, 3)),
            dma((2, 3)),
            dma((2, 3)),
            dma((2, 3)),
            dma((16,)),
            dma((16,)),
        ],
        compiler_params=pltpu.CompilerParams(
            collective_id=0, has_side_effects=True, vmem_limit_bytes=56 << 20
        ),
        name="profile",
    )(traces, primes.reshape(48, 128), family.reshape(4, 128), log_conductor.reshape(4, 128))


def solution(mesh):
    return jax.shard_map(
        on_device,
        mesh=mesh,
        in_specs=(P("curves", "primes"), P("primes"), P("curves"), P("curves")),
        out_specs=P("curves", None),
        check_vma=False,
    )
```

time: 506 us -> 35.3 us (0.07); the launches traced: 498 us -> 35.1 us
  waiting for transfers between devices: 254 us -> 0 us
  blocking collectives: 203 us -> 0 us
  Pallas kernels: 0 us -> 33.8 us
  other arithmetic: 14.8 us -> 0 us
  between operations: 14.1 us -> 0.01 us
  matrix products: 11.3 us -> 0 us
    unnamed x1 -> x0, blocking collectives: 203 us -> none
    reduce_scatter x1 -> x0, waiting for transfers between devices: 200 us -> none  [on_device(): lax.psum_scatter(lax.dot_general(onehot, totals * factor, (((0,), (0,)),...]
    psum x1 -> x0, waiting for transfers between devices: 54.2 us -> none  [on_device(): totals = lax.psum(partial_value, 'primes')]
    pallas_call x0 -> x1, Pallas kernels: none -> 33.8 us  [on_device(): pl.pallas_call(kernel, out_shape=jax.ShapeDtypeStruct((16, 256), F32), in...]
    another operation x1 -> x0, other arithmetic: 12.3 us -> none
    dot_general x2 -> x0, matrix products: 11.3 us -> none  [the longest x1 7.29 us: on_device(): jnp.dot(coefficient, tables, preferred_element_type=jnp.float32)]
  transfers between devices with their start and end apart: 2 -> 0, of which waited for: 2 -> 0; matrix products, arithmetic and copies ran while one was open for 0% -> 0% of each run, Pallas kernels for 0% -> 0%
where the time goes in v1:
time: 35.3 us; the launch traced here: 35.1 us
  Pallas kernels  33.8 us (96%)
  local copies, waits for them, and re-layouts  1.32 us (4%)
    pallas_call x1, Pallas kernels, on_device(): pl.pallas_call(kernel, out_shape=jax.ShapeDtypeStruct((16, 256), F32), in...  33.8 us
    unnamed x1, local copies, waits for them, and re-layouts  1.32 us

profile of v1, /device:TPU:1, one launch (start us, length us, event | category | flops | bytes accessed | tf_op | source)
XLA Modules:
  0.0 35.1 jit_solution(1580676008928225336)
XLA Ops:
  0.0 33.8 %profile.1 = f32[16,256]{1,0:T(8,128)} custom-call(s32[512,6144]{1,0:T(8,128)} %traces.1, s32[48,128]{1,0:T(8,128)} %bitcast.3, s32[4,128]{1,0:T(4,128)} %bitcast.4, f32[4,128]{1,0:T(4,128)} %bitcast.5), custom_call_target="tpu_custom_call" | custom-call | tf_op jit(solution)/shard_map/profile/pallas_call | solution.py:254
  33.8 1.3 %copy.6 = f32[16,256]{1,0:T(8,128)} copy(f32[16,256]{1,0:T(8,128)} %profile.1) | data formatting | bytes 32768

commit v2 on v0

v2 whole, which is shorter than its diff:
```python
import jax
import jax.numpy as jnp
from jax import lax
from jax.experimental import pallas as pl
from jax.experimental.pallas import tpu as pltpu
from jax.sharding import PartitionSpec as P

MESH = pl.DeviceIdType.MESH
ROWS = 512
DEPTH = 6144
CHUNK = 1024
STEPS = DEPTH // CHUNK
GROUPS = CHUNK // 128
FAMILIES = 1024
BLOCK = 256
MEET = 2
F32 = jnp.float32
BF16 = jnp.bfloat16
PIECES = ((0, 0, 32), (1, 0, 32))


def times(a, b):
    return a[0] * b[0] - a[1] * b[1], a[0] * b[1] + a[1] * b[0]


def one_hot(cond):
    return jnp.where(cond, 1.0, 0.0).astype(BF16)


def kernel(
    traces, primes_in, family_in, conductor_in, out,
    tr, primes, family, conductor, inverse, base_cos, base_sin, weight, table, total, factor, hot, rhs, send0, recv0, family2,
    sums, plane_in, column, column_in, count, count_in,
    copy_sem, small_sem, ssem0, rsem0, ssem1, rsem1, ssem2, rsem2, csend, crecv,
):
    me = lax.axis_index("curves")
    zl = lax.axis_index("primes")
    core = lax.rem(me, 2)
    x = lax.rem(lax.div(me, 2), 4)
    zh = lax.rem(lax.div(me, 8), 2)
    y = lax.div(me, 16)

    def curve(y, zh, x, core):
        return ((y * 2 + zh) * 4 + x) * 2 + core

    def in_plane(dx, dy):
        return (curve(lax.rem(y + dy, 4), zh, lax.rem(x + dx, 4), core), zl)

    spot = (zh * 4 + zl) * 2 + core

    def in_column(z_hi, z_lo, k):
        return (curve(y, z_hi, x, k), z_lo)

    sibling = (curve(y, zh, x, 1 - core), zl)

    def remote(src, dst, ssem, rsem, device):
        return pltpu.make_async_remote_copy(src, dst, ssem, rsem, device_id=device, device_id_type=MESH)

    def fetch(i):
        return pltpu.make_async_copy(
            traces.at[:, pl.ds(pl.multiple_of(i * CHUNK, CHUNK), CHUNK)], tr.at[i], copy_sem.at[i]
        )

    def repeat(first, last, do):
        def body(i, carry):
            do(i)
            return carry

        lax.fori_loop(first, last, body, 0)

    small = [
        pltpu.make_async_copy(a, b, small_sem.at[j])
        for j, (a, b) in enumerate(((primes_in, primes), (family_in, family), (conductor_in, conductor)))
    ]
    for copy in small:
        copy.start()
    repeat(0, STEPS, lambda i: fetch(i).start())

    def plane_peer(e):
        return in_plane(lax.rem(e, 4), lax.div(e, 4))

    def column_peer(e):
        q = lax.rem(spot + e, 16)
        return in_column(lax.div(q, 8), lax.rem(lax.div(q, 2), 4), lax.rem(q, 2))

    barrier = pltpu.get_barrier_semaphore()

    def greet(e):
        pl.semaphore_signal(barrier, inc=1, device_id=plane_peer(e), device_id_type=MESH)
        pl.semaphore_signal(barrier, inc=1, device_id=column_peer(e), device_id_type=MESH)

    repeat(1, 16, greet)

    for copy in small:
        copy.wait()

    prime = primes[...].astype(F32)
    log_prime = jnp.log(prime)
    weight[...] = log_prime / prime
    base_cos[...] = jnp.cos(log_prime * 0.5)
    base_sin[...] = jnp.sin(log_prime * 0.5)
    total[...] = jnp.zeros_like(total)

    sub = lax.broadcasted_iota(jnp.int32, (8, 128), 0)
    bits = [(sub & 1) != 0, (sub & 2) != 0, (sub & 4) != 0]

    def pick(mask, a):
        return jnp.where(mask, a[0], 1.0), jnp.where(mask, a[1], 0.0)

    def tables(row, lanes):
        z = (jnp.broadcast_to(base_cos[pl.ds(row, 1), :], (8, 128)), jnp.broadcast_to(base_sin[pl.ds(row, 1), :], (8, 128)))
        z2 = times(z, z)
        z4 = times(z2, z2)
        powers = [times(times(z, pick(bits[0], z)), times(pick(bits[1], z2), pick(bits[2], z4)))]
        step = times(z4, z4)
        for _ in range(4):
            powers = powers + [times(a, step) for a in powers]
            step = times(step, step)
        for part in (0, 1):
            table[part * 128:part * 128 + 128, lanes] = jnp.concatenate([a[part] for a in powers], axis=0).astype(BF16)

    def table_step(j):
        for u in range(2):
            tables(j * 2 + u, pl.ds(pl.multiple_of(j * 256 + u * 128, 128), 128))

    repeat(0, DEPTH // 256, table_step)

    def fill_hot(ref, at):
        def fill(b):
            rows = lax.broadcasted_iota(jnp.int32, (128, 128), 0) + lax.rem(b, 4) * 256 + lax.div(b, 4) * 128
            there = pl.ds(pl.multiple_of(b * 128, 128), 128)
            for g in range(4):
                row = jnp.broadcast_to(ref[g:g + 1, :], (128, 128))
                hot[there, (at + g) * 128:(at + g) * 128 + 128] = one_hot(rows == row)

        repeat(0, 8, fill)

    fill_hot(family, 0)

    inverse[...] = -2.0 / conductor[...]
    count[...] = jnp.zeros_like(count)

    def per_group(g):
        spread = jnp.broadcast_to(inverse[pl.ds(g, 1), :], (128, 128))
        factor[pl.ds(pl.multiple_of(g * 128, 128), 128), :] = jnp.transpose(spread)
        row = family[pl.ds(g, 1), :]
        high = one_hot(lax.broadcasted_iota(jnp.int32, (8, 128), 0) == (row >> 7))
        low = one_hot(lax.broadcasted_iota(jnp.int32, (128, 128), 0) == (row & 127))
        count[0] += lax.dot_general(high, low, (((1,), (1,)), ((), ())), preferred_element_type=F32)

    repeat(0, 4, per_group)

    families = remote(family, family2, ssem0.at[0], rsem0.at[0], sibling)

    def counting(stage, j):
        if stage == 0:
            device = in_plane(j + 1, 0)
        elif stage == 1:
            device = in_plane(0, j + 1)
        else:
            side = (lax.rem(zh + (j + 1) // 2, 2), lax.rem(core + (j + 1) % 2, 2))
            device = in_column(side[0], zl, side[1])
        return remote(count.at[stage], count_in.at[stage, j], csend.at[stage, j], crecv.at[stage, j], device)

    def count_start(stage):
        for j in range(3):
            counting(stage, j).start()

    def count_sum(stage):
        for j in range(3):
            counting(stage, j).wait()
        count[stage + 1] = (count[stage] + count_in[stage, 0]) + (count_in[stage, 1] + count_in[stage, 2])

    def trace_step(i):
        fetch(i).wait()
        w = jnp.concatenate([weight[pl.ds(i * GROUPS + g, 1), :] for g in range(GROUPS)], axis=1)
        coefficient = (tr[i].astype(F32) * w).astype(BF16)
        part = table[:, pl.ds(pl.multiple_of(i * CHUNK, CHUNK), CHUNK)]
        total[...] += lax.dot_general(coefficient, part, (((1,), (1,)), ((), ())), preferred_element_type=F32)

        @pl.when(i == MEET)
        def _():
            pl.semaphore_wait(barrier, 30)
            families.start()
            count_start(0)

        @pl.when(i == STEPS - 2)
        def _():
            families.wait()
            fill_hot(family2, 4)

    repeat(0, STEPS, trace_step)

    def density(k):
        return total[:, pl.ds(pl.multiple_of(k * 128, 128), 128)] * factor[...]

    def split(value, at):
        high = value.astype(BF16)
        rhs[at:at + ROWS, 0:128] = high
        rhs[at:at + ROWS, 128:256] = (value - high.astype(F32)).astype(BF16)

    def add_families(at, columns, fresh):
        there = pl.ds(pl.multiple_of(at, 128), BLOCK)
        both = lax.dot_general(
            hot[there, columns], rhs[columns, :], (((1,), (0,)), ((), ())), preferred_element_type=F32
        )
        value = both[:, 0:128] + both[:, 128:256]
        sums[there, :] = value if fresh else sums[there, :] + value

    send0[...] = density(1 - core)
    columns = remote(send0, recv0, ssem0.at[1], rsem0.at[1], sibling)
    columns.start()
    split(density(core), 0)
    repeat(0, FAMILIES // BLOCK, lambda b: add_families(b * BLOCK, slice(0, 512), True))
    count_sum(0)
    count_start(1)
    columns.wait()
    split(recv0[...], 512)

    mine = y * 4 + x

    def plane_copy(n, e):
        z_hi, first, rows = PIECES[n]
        block = lax.rem(y + lax.div(e, 4), 4) * 4 + lax.rem(x + lax.rem(e, 4), 4)
        at = pl.ds(pl.multiple_of(z_hi * 512 + block * 32 + first, 16), rows)
        return remote(
            sums.at[at, :], plane_in.at[z_hi, e, pl.ds(first, rows), :], ssem1.at[n, e], rsem1.at[n, e], plane_peer(e)
        )

    for n, (z_hi, first, rows) in enumerate(PIECES):
        if first == 0:
            repeat(0, 512 // BLOCK, lambda b: add_families(z_hi * 512 + b * BLOCK, slice(512, 1024), False))
        repeat(1, 16, lambda e: plane_copy(n, e).start())

    def column_copy(n, t):
        z_hi, first, rows = PIECES[n]
        k = lax.rem(t, 2) if rows == 32 else first // 16
        z_lo = lax.div(t, 2) if rows == 32 else t
        there = (z_hi * 4 + z_lo) * 2 + k
        block = column.at[z_hi, pl.ds(pl.multiple_of(k * 16, 16), 16), :]
        copy = remote(block, column_in.at[spot], ssem2.at[there], rsem2.at[spot], in_column(z_hi, z_lo, k))
        return there, copy

    def column_start(n, t):
        there, copy = column_copy(n, t)

        @pl.when(spot != there)
        def _():
            copy.start()

    def column_sent(n, t):
        there, copy = column_copy(n, t)

        @pl.when(spot != there)
        def _():
            copy.wait_send()

    def tree(parts):
        while len(parts) > 1:
            parts = [a + b for a, b in zip(parts[::2], parts[1::2])]
        return parts[0]

    for n, (z_hi, first, rows) in enumerate(PIECES):
        repeat(1, 16, lambda e: plane_copy(n, e).wait_recv())
        at = pl.multiple_of(z_hi * 512 + mine * 32 + first, 16)
        column[z_hi, first:first + rows, :] = tree(
            [sums[pl.ds(at, rows), :]] + [plane_in[z_hi, e, first:first + rows, :] for e in range(1, 16)]
        )
        repeat(0, 8 if rows == 32 else 4, lambda t: column_start(n, t))

    count_sum(1)
    count_start(2)

    column_in[spot] = column[zh, pl.ds(pl.multiple_of(core * 16, 16), 16), :]
    count_sum(2)
    count_row = count[3, pl.ds(lax.div(me, 8), 1), :]
    lane = lax.broadcasted_iota(jnp.int32, (16, 128), 1)
    want = lax.broadcasted_iota(jnp.int32, (16, 128), 0) + lax.rem(me, 8) * 16
    number = jnp.sum(jnp.where(lane == want, jnp.broadcast_to(count_row, (16, 128)), 0.0), axis=1, keepdims=True)
    norm = 1.0 / jnp.sqrt(jnp.maximum(number, 1.0))

    def arrived(t):
        q = lax.rem(spot + t, 16)
        remote(column.at[0, pl.ds(0, 16), :], column_in.at[q], ssem2.at[q], rsem2.at[q], sibling).wait_recv()

    repeat(1, 16, arrived)
    for k in (0, 1):
        out[:, k * 128:k * 128 + 128] = tree([column_in[2 * s + k] for s in range(8)]) * norm

    for n, (z_hi, first, rows) in enumerate(PIECES):
        repeat(0, 8 if rows == 32 else 4, lambda t: column_sent(n, t))
        repeat(1, 16, lambda e: plane_copy(n, e).wait_send())


def on_device(traces, primes, family, log_conductor):
    dma = pltpu.SemaphoreType.DMA
    hbm = pl.BlockSpec(memory_space=pl.ANY)
    return pl.pallas_call(
        kernel,
        out_shape=pltpu.VMEM((16, 256), F32),
        in_specs=[hbm, hbm, hbm, hbm],
        out_specs=pl.BlockSpec(memory_space=pltpu.VMEM),
        scratch_shapes=[
            pltpu.VMEM((STEPS, ROWS, CHUNK), jnp.int32),
            pltpu.VMEM((48, 128), jnp.int32),
            pltpu.VMEM((4, 128), jnp.int32),
            pltpu.VMEM((4, 128), F32),
            pltpu.VMEM((4, 128), F32),
            pltpu.VMEM((48, 128), F32),
            pltpu.VMEM((48, 128), F32),
            pltpu.VMEM((48, 128), F32),
            pltpu.VMEM((256, DEPTH), BF16),
            pltpu.VMEM((ROWS, 256), F32),
            pltpu.VMEM((ROWS, 128), F32),
            pltpu.VMEM((FAMILIES, 1024), BF16),
            pltpu.VMEM((1024, 256), BF16),
            pltpu.VMEM((ROWS, 128), F32),
            pltpu.VMEM((ROWS, 128), F32),
            pltpu.VMEM((4, 128), jnp.int32),
            pltpu.VMEM((FAMILIES, 128), F32),
            pltpu.VMEM((2, 16, 32, 128), F32),
            pltpu.VMEM((2, 32, 128), F32),
            pltpu.VMEM((16, 16, 128), F32),
            pltpu.VMEM((4, 8, 128), F32),
            pltpu.VMEM((3, 3, 8, 128), F32),
            dma((STEPS,)),
            dma((3,)),
            dma((2,)),
            dma((2,)),
            dma((len(PIECES), 16)),
            dma((len(PIECES), 16)),
            dma((16,)),
            dma((16,)),
            dma((3, 3)),
            dma((3, 3)),
        ],
        compiler_params=pltpu.CompilerParams(
            collective_id=0, has_side_effects=True, vmem_limit_bytes=56 << 20
        ),
        name="profile",
    )(traces, primes.reshape(48, 128), family.reshape(4, 128), log_conductor.reshape(4, 128))


def solution(mesh):
    return jax.shard_map(
        on_device,
        mesh=mesh,
        in_specs=(P("curves", "primes"), P("primes"), P("curves"), P("curves")),
        out_specs=P("curves", None),
        check_vma=False,
    )
```

time: 506 us -> 34.2 us (0.07); the launches traced: 498 us -> 34.2 us
  waiting for transfers between devices: 254 us -> 0 us
  blocking collectives: 203 us -> 0 us
  Pallas kernels: 0 us -> 33.5 us
  other arithmetic: 14.8 us -> 0 us
  between operations: 14.1 us -> 0.01 us
  matrix products: 11.3 us -> 0 us
    unnamed x1 -> x0, blocking collectives: 203 us -> none
    reduce_scatter x1 -> x0, waiting for transfers between devices: 200 us -> none  [on_device(): lax.psum_scatter(lax.dot_general(onehot, totals * factor, (((0,), (0,)),...]
    psum x1 -> x0, waiting for transfers between devices: 54.2 us -> none  [on_device(): totals = lax.psum(partial_value, 'primes')]
    pallas_call x0 -> x1, Pallas kernels: none -> 33.5 us  [on_device(): pl.pallas_call(kernel, out_shape=pltpu.VMEM((16, 256), F32), in_specs=[hb...]
    another operation x1 -> x0, other arithmetic: 12.3 us -> none
    dot_general x2 -> x0, matrix products: 11.3 us -> none  [the longest x1 7.29 us: on_device(): jnp.dot(coefficient, tables, preferred_element_type=jnp.float32)]
  transfers between devices with their start and end apart: 2 -> 0, of which waited for: 2 -> 0; matrix products, arithmetic and copies ran while one was open for 0% -> 0% of each run, Pallas kernels for 0% -> 0%
where the time goes in v2:
time: 34.2 us
  Pallas kernels  33.5 us (98%)
  local copies, waits for them, and re-layouts  0.61 us (2%)
    pallas_call x1, Pallas kernels, on_device(): pl.pallas_call(kernel, out_shape=pltpu.VMEM((16, 256), F32), in_specs=[hb...  33.5 us

profile of v2, /device:TPU:1, one launch (start us, length us, event | category | flops | bytes accessed | tf_op | source)
XLA Modules:
  0.0 34.2 jit_solution(10871445519473902891)
XLA Ops:
  0.0 33.5 %profile.1 = f32[16,256]{1,0:T(8,128)S(1)} custom-call(s32[512,6144]{1,0:T(8,128)} %traces.1, s32[48,128]{1,0:T(8,128)} %bitcast.3, s32[4,128]{1,0:T(4,128)} %bitcast.4, f32[4,128]{1,0:T(4,128)} %bitcast.5), custom_call_target="tpu_custom_call" | custom-call | tf_op jit(solution)/shard_map/profile/pallas_call | solution.py:298
  33.5 0.6 %copy.6 = f32[16,256]{1,0:T(8,128)} copy(f32[16,256]{1,0:T(8,128)S(1)} %profile.1) | data formatting | bytes 32768

commit v3 on v2

--- a/solution.py
+++ b/solution.py
@@ -16,7 +16,8 @@
 MEET = 2
 F32 = jnp.float32
 BF16 = jnp.bfloat16
-PIECES = ((0, 0, 32), (1, 0, 32))
+PIECES = (0, 1)
+ROTATE = 0
 
 
 def times(a, b):
@@ -219,26 +220,53 @@
 
     mine = y * 4 + x
 
-    def plane_copy(n, e):
-        z_hi, first, rows = PIECES[n]
-        block = lax.rem(y + lax.div(e, 4), 4) * 4 + lax.rem(x + lax.rem(e, 4), 4)
-        at = pl.ds(pl.multiple_of(z_hi * 512 + block * 32 + first, 16), rows)
-        return remote(
-            sums.at[at, :], plane_in.at[z_hi, e, pl.ds(first, rows), :], ssem1.at[n, e], rsem1.at[n, e], plane_peer(e)
+    def plane_copy(n, i):
+        z_hi = PIECES[n]
+        b = lax.rem(i + ROTATE * mine, 16)
+        at = pl.ds(pl.multiple_of(z_hi * 512 + b * 32, 32), 32)
+        copy = remote(
+            sums.at[at, :], plane_in.at[z_hi, mine], ssem1.at[n, b], rsem1.at[n, mine],
+            (curve(lax.div(b, 4), zh, lax.rem(b, 4), core), zl),
         )
-
-    for n, (z_hi, first, rows) in enumerate(PIECES):
-        if first == 0:
-            repeat(0, 512 // BLOCK, lambda b: add_families(z_hi * 512 + b * BLOCK, slice(512, 1024), False))
-        repeat(1, 16, lambda e: plane_copy(n, e).start())
+        return b, copy
+
+    def plane_start(n, i):
+        b, copy = plane_copy(n, i)
+
+        @pl.when(b != mine)
+        def _():
+            copy.start()
+
+    def plane_arrived(n, b):
+        here = plane_in.at[PIECES[n], b]
+
+        @pl.when(b != mine)
+        def _():
+            remote(here, here, ssem1.at[n, b], rsem1.at[n, b], sibling).wait_recv()
+
+    def plane_sent(n, i):
+        b, copy = plane_copy(n, i)
+
+        @pl.when(b != mine)
+        def _():
+            copy.wait_send()
+
+    def plane_scatter(n):
+        z_hi = PIECES[n]
+        repeat(0, 16, lambda i: plane_start(n, i))
+        plane_in[z_hi, mine] = sums[pl.ds(pl.multiple_of(z_hi * 512 + mine * 32, 32), 32), :]
+
+    def finish_families(n):
+        repeat(0, 512 // BLOCK, lambda b: add_families(PIECES[n] * 512 + b * BLOCK, slice(512, 1024), False))
 
     def column_copy(n, t):
-        z_hi, first, rows = PIECES[n]
-        k = lax.rem(t, 2) if rows == 32 else first // 16
-        z_lo = lax.div(t, 2) if rows == 32 else t
-        there = (z_hi * 4 + z_lo) * 2 + k
+        z_hi = PIECES[n]
+        k = 1 - lax.rem(t, 2)
+        there = z_hi * 8 + lax.div(t, 2) * 2 + k
         block = column.at[z_hi, pl.ds(pl.multiple_of(k * 16, 16), 16), :]
-        copy = remote(block, column_in.at[spot], ssem2.at[there], rsem2.at[spot], in_column(z_hi, z_lo, k))
+        copy = remote(
+            block, column_in.at[spot], ssem2.at[there], rsem2.at[spot], in_column(z_hi, lax.div(t, 2), k)
+        )
         return there, copy
 
     def column_start(n, t):
@@ -260,16 +288,20 @@
             parts = [a + b for a, b in zip(parts[::2], parts[1::2])]
         return parts[0]
 
-    for n, (z_hi, first, rows) in enumerate(PIECES):
-        repeat(1, 16, lambda e: plane_copy(n, e).wait_recv())
-        at = pl.multiple_of(z_hi * 512 + mine * 32 + first, 16)
-        column[z_hi, first:first + rows, :] = tree(
-            [sums[pl.ds(at, rows), :]] + [plane_in[z_hi, e, first:first + rows, :] for e in range(1, 16)]
-        )
-        repeat(0, 8 if rows == 32 else 4, lambda t: column_start(n, t))
-
+    def plane_gather(n):
+        z_hi = PIECES[n]
+        repeat(0, 16, lambda b: plane_arrived(n, b))
+        column[z_hi] = tree([plane_in[z_hi, b] for b in range(16)])
+        repeat(0, 8, lambda t: column_start(n, t))
+
+    finish_families(0)
+    plane_scatter(0)
+    finish_families(1)
     count_sum(1)
     count_start(2)
+    plane_gather(0)
+    plane_scatter(1)
+    plane_gather(1)
 
     column_in[spot] = column[zh, pl.ds(pl.multiple_of(core * 16, 16), 16), :]
     count_sum(2)
@@ -287,9 +319,9 @@
     for k in (0, 1):
         out[:, k * 128:k * 128 + 128] = tree([column_in[2 * s + k] for s in range(8)]) * norm
 
-    for n, (z_hi, first, rows) in enumerate(PIECES):
-        repeat(0, 8 if rows == 32 else 4, lambda t: column_sent(n, t))
-        repeat(1, 16, lambda e: plane_copy(n, e).wait_send())
+    for n in range(2):
+        repeat(0, 8, lambda t: column_sent(n, t))
+        repeat(0, 16, lambda i: plane_sent(n, i))
 
 
 def on_device(traces, primes, family, log_conductor):

time: 34.2 us -> 29.1 us (0.85); the launches traced: 34.2 us -> 28.6 us
  Pallas kernels: 33.5 us -> 28 us
    pallas_call x1, Pallas kernels: 33.5 us -> 28 us  [on_device(): pl.pallas_call(kernel, out_shape=pltpu.VMEM((16, 256), F32), in_specs=[hb...]
where the time goes in v3:
time: 29.1 us; the launch traced here: 28.6 us
  Pallas kernels  28 us (96%)
  local copies, waits for them, and re-layouts  0.61 us (2%)
    pallas_call x1, Pallas kernels, on_device(): pl.pallas_call(kernel, out_shape=pltpu.VMEM((16, 256), F32), in_specs=[hb...  28 us
    unnamed x1, local copies, waits for them, and re-layouts  0.61 us

profile of v3, /device:TPU:1, one launch (start us, length us, event | category | flops | bytes accessed | tf_op | source)
XLA Modules:
  0.0 28.6 jit_solution(6385143855104497001)
XLA Ops:
  0.0 28.0 %profile.1 = f32[16,256]{1,0:T(8,128)S(1)} custom-call(s32[512,6144]{1,0:T(8,128)} %traces.1, s32[48,128]{1,0:T(8,128)} %bitcast.3, s32[4,128]{1,0:T(4,128)} %bitcast.4, f32[4,128]{1,0:T(4,128)} %bitcast.5), custom_call_target="tpu_custom_call" | custom-call | tf_op jit(solution)/shard_map/profile/pallas_call | solution.py:330
  28.0 0.6 %copy.6 = f32[16,256]{1,0:T(8,128)} copy(f32[16,256]{1,0:T(8,128)S(1)} %profile.1) | data formatting | bytes 32768

commit v4 on v3

--- a/solution.py
+++ b/solution.py
@@ -8,12 +8,12 @@
 MESH = pl.DeviceIdType.MESH
 ROWS = 512
 DEPTH = 6144
-CHUNK = 1024
+CHUNK = 2048
 STEPS = DEPTH // CHUNK
 GROUPS = CHUNK // 128
 FAMILIES = 1024
 BLOCK = 256
-MEET = 2
+MEET = 1
 F32 = jnp.float32
 BF16 = jnp.bfloat16
 PIECES = (0, 1)
@@ -185,11 +185,6 @@
             families.start()
             count_start(0)
 
-        @pl.when(i == STEPS - 2)
-        def _():
-            families.wait()
-            fill_hot(family2, 4)
-
     repeat(0, STEPS, trace_step)
 
     def density(k):
@@ -213,6 +208,8 @@
     columns.start()
     split(density(core), 0)
     repeat(0, FAMILIES // BLOCK, lambda b: add_families(b * BLOCK, slice(0, 512), True))
+    families.wait()
+    fill_hot(family2, 4)
     count_sum(0)
     count_start(1)
     columns.wait()

time: 29.1 us -> 28.6 us (0.983)
  the two profiles are of different devices: /device:TPU:1 before, /device:TPU:224 now
where the time goes in v4:
time: 28.6 us
  Pallas kernels  27.9 us (98%)
  local copies, waits for them, and re-layouts  0.61 us (2%)
    pallas_call x1, Pallas kernels, on_device(): pl.pallas_call(kernel, out_shape=pltpu.VMEM((16, 256), F32), in_specs=[hb...  27.9 us
    unnamed x1, local copies, waits for them, and re-layouts  0.61 us

profile of v4, /device:TPU:224, one launch (start us, length us, event | category | flops | bytes accessed | tf_op | source)
XLA Modules:
  0.0 28.6 jit_solution(7900337147640430945)
XLA Ops:
  0.0 27.9 %profile.1 = f32[16,256]{1,0:T(8,128)S(1)} custom-call(s32[512,6144]{1,0:T(8,128)} %traces.1, s32[48,128]{1,0:T(8,128)} %bitcast.3, s32[4,128]{1,0:T(4,128)} %bitcast.4, f32[4,128]{1,0:T(4,128)} %bitcast.5), custom_call_target="tpu_custom_call" | custom-call | tf_op jit(solution)/shard_map/profile/pallas_call | solution.py:327
  27.9 0.6 %copy.6 = f32[16,256]{1,0:T(8,128)} copy(f32[16,256]{1,0:T(8,128)S(1)} %profile.1) | data formatting | bytes 32768

commit v5 on v4

--- a/solution.py
+++ b/solution.py
@@ -30,7 +30,7 @@
 
 def kernel(
     traces, primes_in, family_in, conductor_in, out,
-    tr, primes, family, conductor, inverse, base_cos, base_sin, weight, table, total, factor, hot, rhs, send0, recv0, family2,
+    tr, primes, family, conductor, base_cos, base_sin, weight, table, total, factor, hot, rhs, send0, recv0, family2,
     sums, plane_in, column, column_in, count, count_in,
     copy_sem, small_sem, ssem0, rsem0, ssem1, rsem1, ssem2, rsem2, csend, crecv,
 ):
@@ -138,18 +138,14 @@
 
     fill_hot(family, 0)
 
-    inverse[...] = -2.0 / conductor[...]
-    count[...] = jnp.zeros_like(count)
-
-    def per_group(g):
-        spread = jnp.broadcast_to(inverse[pl.ds(g, 1), :], (128, 128))
-        factor[pl.ds(pl.multiple_of(g * 128, 128), 128), :] = jnp.transpose(spread)
-        row = family[pl.ds(g, 1), :]
-        high = one_hot(lax.broadcasted_iota(jnp.int32, (8, 128), 0) == (row >> 7))
-        low = one_hot(lax.broadcasted_iota(jnp.int32, (128, 128), 0) == (row & 127))
-        count[0] += lax.dot_general(high, low, (((1,), (1,)), ((), ())), preferred_element_type=F32)
-
-    repeat(0, 4, per_group)
+    inverse = -2.0 / conductor[...]
+    for g in range(4):
+        factor[g * 128:g * 128 + 128, :] = jnp.transpose(jnp.broadcast_to(inverse[g:g + 1, :], (128, 128)))
+
+    row = jnp.concatenate([family[g:g + 1, :] for g in range(4)], axis=1)
+    high = one_hot(lax.broadcasted_iota(jnp.int32, (8, ROWS), 0) == (row >> 7))
+    low = one_hot(lax.broadcasted_iota(jnp.int32, (128, ROWS), 0) == (row & 127))
+    count[0] = lax.dot_general(high, low, (((1,), (1,)), ((), ())), preferred_element_type=F32)
 
     families = remote(family, family2, ssem0.at[0], rsem0.at[0], sibling)
 
@@ -312,13 +308,12 @@
         q = lax.rem(spot + t, 16)
         remote(column.at[0, pl.ds(0, 16), :], column_in.at[q], ssem2.at[q], rsem2.at[q], sibling).wait_recv()
 
+    for n in range(len(PIECES)):
+        repeat(0, 16, lambda i: plane_sent(n, i))
+        repeat(0, 8, lambda t: column_sent(n, t))
     repeat(1, 16, arrived)
     for k in (0, 1):
         out[:, k * 128:k * 128 + 128] = tree([column_in[2 * s + k] for s in range(8)]) * norm
-
-    for n in range(2):
-        repeat(0, 8, lambda t: column_sent(n, t))
-        repeat(0, 16, lambda i: plane_sent(n, i))
 
 
 def on_device(traces, primes, family, log_conductor):
@@ -333,7 +328,6 @@
             pltpu.VMEM((STEPS, ROWS, CHUNK), jnp.int32),
             pltpu.VMEM((48, 128), jnp.int32),
             pltpu.VMEM((4, 128), jnp.int32),
-            pltpu.VMEM((4, 128), F32),
             pltpu.VMEM((4, 128), F32),
             pltpu.VMEM((48, 128), F32),
             pltpu.VMEM((48, 128), F32),

time: 28.6 us -> 27.8 us (0.972)
  the two profiles are of different devices: /device:TPU:224 before, /device:TPU:1 now
where the time goes in v5:
time: 27.8 us; the launch traced here: 27.3 us
  Pallas kernels  26.6 us (96%)
  local copies, waits for them, and re-layouts  0.61 us (2%)
    pallas_call x1, Pallas kernels, on_device(): pl.pallas_call(kernel, out_shape=pltpu.VMEM((16, 256), F32), in_specs=[hb...  26.6 us
    unnamed x1, local copies, waits for them, and re-layouts  0.61 us

profile of v5, /device:TPU:1, one launch (start us, length us, event | category | flops | bytes accessed | tf_op | source)
XLA Modules:
  0.0 27.3 jit_solution(2402011915943831156)
XLA Ops:
  0.0 26.6 %profile.1 = f32[16,256]{1,0:T(8,128)S(1)} custom-call(s32[512,6144]{1,0:T(8,128)} %traces.1, s32[48,128]{1,0:T(8,128)} %bitcast.3, s32[4,128]{1,0:T(4,128)} %bitcast.4, f32[4,128]{1,0:T(4,128)} %bitcast.5), custom_call_target="tpu_custom_call" | custom-call | tf_op jit(solution)/shard_map/profile/pallas_call | solution.py:322
  26.6 0.6 %copy.6 = f32[16,256]{1,0:T(8,128)} copy(f32[16,256]{1,0:T(8,128)S(1)} %profile.1) | data formatting | bytes 32768

commit v6 on v5

--- a/solution.py
+++ b/solution.py
@@ -12,7 +12,7 @@
 STEPS = DEPTH // CHUNK
 GROUPS = CHUNK // 128
 FAMILIES = 1024
-BLOCK = 256
+BLOCK = 512
 MEET = 1
 F32 = jnp.float32
 BF16 = jnp.bfloat16

time: 27.8 us -> 27.7 us (level)
  no operation moved by 1% of the time
where the time goes in v6:
time: 27.7 us; the launch traced here: 27.2 us
  Pallas kernels  26.6 us (96%)
  local copies, waits for them, and re-layouts  0.61 us (2%)
    pallas_call x1, Pallas kernels, on_device(): pl.pallas_call(kernel, out_shape=pltpu.VMEM((16, 256), F32), in_specs=[hb...  26.6 us
    unnamed x1, local copies, waits for them, and re-layouts  0.61 us

profile of v6, /device:TPU:1, one launch (start us, length us, event | category | flops | bytes accessed | tf_op | source)
XLA Modules:
  0.0 27.2 jit_solution(3652491316224214047)
XLA Ops:
  0.0 26.6 %profile.1 = f32[16,256]{1,0:T(8,128)S(1)} custom-call(s32[512,6144]{1,0:T(8,128)} %traces.1, s32[48,128]{1,0:T(8,128)} %bitcast.3, s32[4,128]{1,0:T(4,128)} %bitcast.4, f32[4,128]{1,0:T(4,128)} %bitcast.5), custom_call_target="tpu_custom_call" | custom-call | tf_op jit(solution)/shard_map/profile/pallas_call | solution.py:322
  26.6 0.6 %copy.6 = f32[16,256]{1,0:T(8,128)} copy(f32[16,256]{1,0:T(8,128)S(1)} %profile.1) | data formatting | bytes 32768
